TPU v7x, 256 devices: a whole 4x4x8 slice. The times are simulated.
256 devices in a mesh: wide: 128 (over y, z, x), cols: 2 (over core).
Axes of the slice: x: 4, y: 4, z: 8, core: 2. Of those that a mesh axis runs over, the one named last changes fastest.
Arguments:
- factor: float32 [262144, 256], P('wide', 'cols')
- gates: float32 [8, 128, 128], replicated, may hold values from -0.5 to 0.5
- gate_layout: int32 [2048], P('wide'), may hold values from 0 to 7
- jump_masks: int32 [3], replicated, may hold values from 1 to 127
- jump_rates: float32 [3], replicated, may hold values from 0.1 to 0.4
- sketch_perm: int32 [1024], replicated, may hold values from 0 to 1023, each once
- bases: float32 [8, 64, 64], replicated, may hold values from -0.75 to 0.75
- basis_index: int32 [128, 32], P('wide'), may hold values from 0 to 7
Outputs:
- new_factor: float32 [262144, 256], P('wide', 'cols')
- weights: float32 [128, 2048], P('wide', 'cols')
Inputs may be any that keep to these rules, and one draw needn't show every extreme that they name: `jump_masks`: nonzero bit masks over the high qubits. `sketch_perm`: each value appears once.
All inputs are finite; a program needn't handle non-finite values.
Results may differ from a plain program's by a relative error of at most 0.0003.
Values sent between devices are 32-bit elements; how exact they have to be, the bound alone decides.
No kernel may reach another device: no remote copies, remote signals or barrier semaphores. Data moves between devices by JAX's collectives and lax.ppermute only.
A program may use at most 64 MiB of HBM per device.

v0:
```python
import jax
import jax.numpy as jnp
from jax import lax
from jax.sharding import PartitionSpec as P

NS_ITERS = 7
HIGH = lax.Precision.HIGHEST


def apply_blocks(mats, index, data):
    chosen = jnp.take(mats, index, axis=0)
    return jnp.einsum("bij,bjc->bic", chosen, data, precision=HIGH)


def flip_rows(data, mask, count):
    shaped = data.reshape(count, data.shape[0] // count, data.shape[1])
    source = jnp.bitwise_xor(jnp.arange(count, dtype=jnp.int32), mask)
    return jnp.take(shaped, source, axis=0).reshape(data.shape)


def sketch_table(sketch_perm, rank):
    target = sketch_perm % rank
    sign = 1.0 - 2.0 * (sketch_perm // rank % 2).astype(jnp.float32)
    hit = target[:, None] == jnp.arange(rank, dtype=jnp.int32)[None, :]
    return jnp.where(hit, sign[:, None], jnp.zeros((), jnp.float32))


def mixed_stack(source, table, first, coefs, masks, count):
    rank = table.shape[1]
    width = source.shape[1]
    sources = []
    blocks = []
    for k in range(len(coefs)):
        flipped = source if k == 0 else flip_rows(source, masks[k - 1], count)
        sources.append(coefs[k] * flipped)
        blocks.append(lax.dynamic_slice_in_dim(table, k * rank + first, width, 0))
    joined = jnp.concatenate(sources, axis=1)
    table_rows = jnp.concatenate(blocks, axis=0)
    return jnp.dot(joined, table_rows, precision=HIGH, preferred_element_type=jnp.float32)


def newton_root(mat, eye, iters):
    fro = jnp.sqrt(jnp.sum(mat * mat))
    approx = mat / (fro + 1e-06)
    inverse = eye
    for step in range(iters):
        middle = 1.5 * eye - 0.5 * jnp.dot(inverse, approx, precision=HIGH)
        approx = jnp.dot(approx, middle, precision=HIGH)
        inverse = jnp.dot(middle, inverse, precision=HIGH)
    return (approx, inverse, fro)


def per_device(factor, gates, gate_layout, jump_masks, jump_rates, sketch_perm, bases, basis_index):
    rows, width = factor.shape
    order = gates.shape[1]
    count = lax.axis_size("wide")
    halves = lax.axis_size("cols")
    column_index = lax.axis_index("cols")
    rank = width * halves
    jumps = jump_rates.shape[0]
    gated = apply_blocks(gates, gate_layout, factor.reshape(rows // order, order, width)).reshape(
        rows, width
    )
    moved = lax.all_to_all(gated, "wide", split_axis=0, concat_axis=0, tiled=True)
    keep = 1.0 - 0.5 * jnp.sum(jump_rates)
    coefs = [keep] + [jnp.sqrt(jump_rates[k]) for k in range(jumps)]
    table = sketch_table(sketch_perm, rank)
    first = column_index * width
    terms = mixed_stack(moved, table, first, coefs, jump_masks, count)
    sketch_own = lax.psum_scatter(terms, "cols", scatter_dimension=1, tiled=True)
    sketch = lax.all_gather(sketch_own, "cols", axis=1, tiled=True)
    share = rows // halves
    mine = lax.dynamic_slice_in_dim(sketch, column_index * share, share, 0)
    gram_part = lax.dot_general(
        mine, mine, (((0,), (0,)), ((), ())), precision=HIGH, preferred_element_type=jnp.float32
    )
    gram = lax.psum(gram_part, ("wide", "cols"))
    eye = jnp.eye(rank, dtype=jnp.float32)
    unused, inverse, fro = newton_root(gram, eye, NS_ITERS)
    parts = []
    for k in range(jumps + 1):
        right = moved if k == 0 else flip_rows(moved, jump_masks[k - 1], count)
        parts.append(
            coefs[k]
            * lax.dot_general(
                sketch,
                right,
                (((0,), (0,)), ((), ())),
                precision=HIGH,
                preferred_element_type=jnp.float32,
            )
        )
    proj_own = jnp.concatenate(parts, axis=1)
    proj_sum = lax.psum(proj_own, "wide")
    coeff = lax.dot_general(
        inverse,
        proj_sum,
        (((0,), (0,)), ((), ())),
        precision=HIGH,
        preferred_element_type=jnp.float32,
    )
    core_part = lax.dot_general(
        coeff, coeff, (((1,), (1,)), ((), ())), precision=HIGH, preferred_element_type=jnp.float32
    )
    core = lax.psum(core_part, "cols")
    approx_two, unused_two, fro_two = newton_root(core, eye, NS_ITERS)
    root_own = jnp.sqrt(fro_two + 1e-06) * lax.dynamic_slice_in_dim(approx_two, first, width, 1)
    mixing_own = jnp.dot(inverse, root_own, precision=HIGH)
    new_own = jnp.dot(sketch, mixing_own, precision=HIGH)
    rot = bases.shape[1]
    rotated = apply_blocks(bases, basis_index.reshape(-1), new_own.reshape(rows // rot, rot, width))
    partial_value = (jnp.sum(rotated * rotated, axis=2) / rank).reshape(1, rows)
    weights = lax.psum_scatter(partial_value, "cols", scatter_dimension=1, tiled=True)
    return (new_own, weights)


def solution(mesh):
    return jax.shard_map(
        per_device,
        mesh=mesh,
        in_specs=(P("wide", "cols"), P(), P("wide"), P(), P(), P(), P(), P("wide", None)),
        out_specs=(P("wide", "cols"), P("wide", "cols")),
        check_vma=False,
    )
```

profile of v0, /device:TPU:1, one launch (start us, length us, event | category | flops | bytes accessed | tf_op | source)
XLA Modules:
  0.0 657.7 jit_solution(18310592391966807667)
XLA Ops:
  8.6 1.7 gather_fusion
  10.3 2.2 fusion.12
  12.5 16.3 %all-to-all-start = ((f32[128,16,128]{2,1,0:T(8,128)}), f32[128,16,128]{2,1,0:T(8,128)S(1)}, u32[]{:S(2)}, u32[]{:S(2)}) async-start(f32[128,16,128]{2,1,0:T(8,128)} %bitcast.1), calls=%async_computation | async-start | bytes 2097152 | tf_op jit(solution)/shard_map/all_to_all | solution.py:64
  36.7 1.8 compare_and_fusion
  39.6 16.5 %all-to-all-done = f32[128,16,128]{2,1,0:T(8,128)S(1)} async-done(((f32[128,16,128]{2,1,0:T(8,128)}), f32[128,16,128]{2,1,0:T(8,128)S(1)}, u32[]{:S(2)}, u32[]{:S(2)}) %all-to-all-start) | async-done | bytes 1048608 | tf_op jit(solution)/shard_map/all_to_all | solution.py:64
  65.7 4.9 fusion
  70.6 13.1 %reduce-scatter.5.cloned.1.call-done = f32[2048,128]{1,0:T(8,128)} async-done(((f32[2048,256]{1,0:T(8,128)}), f32[2048,128]{1,0:T(8,128)}) %reduce-scatter.5.cloned.1.call-update) | async-done | bytes 1048592 | tf_op jit(solution)/shard_map/reduce_scatter | solution.py:70
  83.8 19.0 %all-gather.2.cloned.1.call-done = f32[2048,256]{1,0:T(8,128)} async-done(((f32[2048,128]{1,0:T(8,128)}), f32[2048,256]{1,0:T(8,128)}) %all-gather.2.cloned.1.call-update) | async-done | bytes 2097168 | tf_op jit(solution)/shard_map/all_gather | solution.py:71
  102.7 4.1 fusion.10
  107.4 5.4 convolution_multiply_fusion.16
  112.8 3.4 convolution_multiply_fusion.15
  116.3 3.4 convolution_multiply_fusion.17
  119.7 3.6 convolution_multiply_fusion.18
  124.2 234.4 %all-reduce.4.cloned.1.call-done = f32[256,256]{1,0:T(8,128)} async-done(((f32[256,256]{1,0:T(8,128)}), f32[256,256]{1,0:T(8,128)}) %all-reduce.4.cloned.1.call-update) | async-done | bytes 262160 | tf_op jit(solution)/shard_map/psum | solution.py:77
  358.6 1.6 multiply_reduce_fusion.1
  371.1 206.0 %all-reduce.6.cloned.1.call-done = f32[256,512]{1,0:T(8,128)} async-done(((f32[256,512]{1,0:T(8,128)}), f32[256,512]{1,0:T(8,128)}) %all-reduce.6.cloned.1.call-update) | async-done | bytes 524304 | tf_op jit(solution)/shard_map/psum | solution.py:94
  577.2 1.7 fusion.59
  580.6 1.6 gather_fusion.1
  582.2 30.0 %all-reduce.8.cloned.1.call-done = f32[256,256]{1,0:T(8,128)} async-done(((f32[256,256]{1,0:T(8,128)}), f32[256,256]{1,0:T(8,128)}) %all-reduce.8.cloned.1.call-update) | async-done | bytes 262160 | tf_op jit(solution)/shard_map/psum | solution.py:105
  612.2 1.6 multiply_reduce_fusion
  627.1 1.8 fusion.72
  631.5 2.0 div.43
  633.5 15.3 %reduce-scatter.7.cloned.1.call-done = f32[1024,1]{1,0:T(8,128)} async-done(((f32[2048,1]{1,0:T(8,128)}), f32[1024,1]{1,0:T(8,128)}) %reduce-scatter.7.cloned.1.call-update) | async-done | bytes 4112
  648.8 1.8 copy.11
  (125 shorter events, 45.2 us)
Async XLA Ops:
  7.2 3.1 copy-start
  10.3 18.6 %copy-start.16 = (f32[3]{0:T(128)S(1)}, f32[3]{0:T(128)}, u32[]{:S(2)}) copy-start(f32[3]{0:T(128)} %param.14) | copy-start | bytes 40
  10.3 22.6 %copy-start.17 = (s32[3]{0:T(128)S(1)}, s32[3]{0:T(128)}, u32[]{:S(2)}) copy-start(s32[3]{0:T(128)} %param.13) | copy-start | bytes 40
  10.3 28.2 %copy-start.15 = (s32[1024]{0:T(1024)S(1)}, s32[1024]{0:T(1024)}, u32[]{:S(2)}) copy-start(s32[1024]{0:T(1024)} %param.15) | copy-start | bytes 12292
  12.5 43.6 %all-to-all-start = ((f32[128,16,128]{2,1,0:T(8,128)}), f32[128,16,128]{2,1,0:T(8,128)S(1)}, u32[]{:S(2)}, u32[]{:S(2)}) async-start(f32[128,16,128]{2,1,0:T(8,128)} %bitcast.1), calls=%async_computation | async-start | bytes 2097152 | tf_op jit(solution)/shard_map/all_to_all | solution.py:64
  28.8 54.8 %reduce-scatter.5.cloned.1.call-start = ((), (), s32[]{:S(2)}) async-start(), calls=%async_computation.3 | async-start | bytes 3145728 | tf_op jit(solution)/shard_map/reduce_scatter | solution.py:70
  56.1 7.7 %copy-start.2 = (f32[128,16,128]{2,1,0:T(8,128)}, f32[128,16,128]{2,1,0:T(8,128)S(1)}, u32[]{:S(2)}) copy-start(f32[128,16,128]{2,1,0:T(8,128)S(1)} %all-to-all-done) | copy-start | bytes 3145732
  61.7 1.8 copy-start.18
  63.7 1.0 copy-start.7
  63.7 1.6 copy-start.12
  63.8 1.9 copy-start.13
  63.8 1.9 copy-start.14
  70.5 13.2 %copy-start.19 = (s32[1,32]{1,0:T(1,128)S(1)}, s32[1,32]{1,0:T(1,128)}, u32[]{:S(2)}) copy-start(s32[1,32]{1,0:T(1,128)} %param.17) | copy-start | bytes 388
  70.6 32.2 %all-gather.2.cloned.1.call-start = ((), (), s32[]{:S(2)}) async-start(), calls=%async_computation.4 | async-start | bytes 3145728 | tf_op jit(solution)/shard_map/all_gather | solution.py:71
  83.7 274.9 %all-reduce.4.cloned.1.call-start = ((), (), s32[]{:S(2)}) async-start(), calls=%async_computation.5 | async-start | bytes 524288 | tf_op jit(solution)/shard_map/psum | solution.py:77
  106.9 5.9 copy-start.1
  106.9 470.3 %all-reduce.6.cloned.1.call-start = ((), (), s32[]{:S(2)}) async-start(), calls=%async_computation.6 | async-start | bytes 1048576 | tf_op jit(solution)/shard_map/psum | solution.py:94
  107.4 5.4 copy-start.6
  112.8 3.5 copy-start.8
  116.3 3.5 copy-start.3
  124.2 488.0 %all-reduce.8.cloned.1.call-start = ((), (), s32[]{:S(2)}) async-start(), calls=%async_computation.7 | async-start | bytes 524288 | tf_op jit(solution)/shard_map/psum | solution.py:105
  369.6 210.9 %copy-start.11 = (f32[8,64,64]{2,1,0:T(8,128)S(1)}, f32[8,64,64]{2,1,0:T(8,128)}, u32[]{:S(2)}) copy-start(f32[8,64,64]{2,1,0:T(8,128)} %param.16) | copy-start | bytes 393220
  580.3 68.5 %reduce-scatter.7.cloned.1.call-start = ((), (), s32[]{:S(2)}) async-start(), calls=%async_computation.8 | async-start | bytes 1572864
  625.7 4.3 copy-start.10
  (3 other events, 2.9 us)
Sparse Core Ops, SparseCore 0:
  70.7 12.9 reduce-scatter.4
  85.6 17.0 all-gather.1
  109.1 249.4 all-reduce.3
  365.3 211.7 all-reduce.5
  580.4 31.7 all-reduce.7
  633.6 15.1 reduce-scatter.6
where the time goes:
time: 666 us; the launch traced here: 658 us
  waiting for transfers between devices  534 us (80%)
  matrix products  55.9 us (8%)
  between operations  19.3 us (3%)
  starting transfers between devices  17.3 us (3%)
  local copies, waits for them, and re-layouts  16.1 us (2%)
  other arithmetic  14.9 us (2%)
    psum x1, waiting for transfers between devices, per_device(): gram = lax.psum(gram_part, ('wide', 'cols'))  234 us
    psum x1, waiting for transfers between devices, per_device(): proj_sum = lax.psum(proj_own, 'wide')  206 us
    psum x1, waiting for transfers between devices, per_device(): core = lax.psum(core_part, 'cols')  30 us
    all_gather x1, waiting for transfers between devices, per_device(): sketch = lax.all_gather(sketch_own, 'cols', axis=1, tiled=True)  19 us
    all_to_all x1, waiting for transfers between devices, per_device(): lax.all_to_all(gated, 'wide', split_axis=0, concat_axis=0, tiled=True)  16.5 us
    all_to_all x1, starting transfers between devices, per_device(): lax.all_to_all(gated, 'wide', split_axis=0, concat_axis=0, tiled=True)  16.3 us
    dot_general x4, matrix products, per_device(): lax.dot_general(sketch, right, (((0,), (0,)), ((), ())), precision=HIGH,...  15.9 us
    unnamed x7, waiting for transfers between devices  15.4 us
  transfers between devices with their start and end apart: 7, of which 7 were waited for; matrix products, arithmetic and copies ran while one was open for 6% of the time, Pallas kernels for 0%

commit v1 on v0

--- a/solution.py
+++ b/solution.py
@@ -74,7 +74,9 @@
     gram_part = lax.dot_general(
         mine, mine, (((0,), (0,)), ((), ())), precision=HIGH, preferred_element_type=jnp.float32
     )
-    gram = lax.psum(gram_part, ("wide", "cols"))
+    gram = gram_part
+    for i0 in ("cols", "wide"):
+        gram = lax.psum(gram, axis_name=i0)
     eye = jnp.eye(rank, dtype=jnp.float32)
     unused, inverse, fro = newton_root(gram, eye, NS_ITERS)
     parts = []

time: 666 us -> 459 us (0.69)
  waiting for transfers between devices: 534 us -> 328 us
    psum x2, waiting for transfers between devices: 440 us -> 234 us  [per_device(): gram = lax.psum(gram, axis_name=i0)]
where the time goes in v1:
time: 459 us; the launch traced here: 450 us
  waiting for transfers between devices  328 us (71%)
  matrix products  54 us (12%)
  between operations  19.2 us (4%)
  starting transfers between devices  17.3 us (4%)
  local copies, waits for them, and re-layouts  16.8 us (4%)
  other arithmetic  14.8 us (3%)
    psum x2, waiting for transfers between devices, per_device(): gram = lax.psum(gram, axis_name=i0)  234 us
    psum x1, waiting for transfers between devices, per_device(): core = lax.psum(core_part, 'cols')  29.8 us
    all_gather x1, waiting for transfers between devices, per_device(): sketch = lax.all_gather(sketch_own, 'cols', axis=1, tiled=True)  19 us
    all_to_all x1, waiting for transfers between devices, per_device(): lax.all_to_all(gated, 'wide', split_axis=0, concat_axis=0, tiled=True)  16.6 us
    all_to_all x1, starting transfers between devices, per_device(): lax.all_to_all(gated, 'wide', split_axis=0, concat_axis=0, tiled=True)  16.3 us
    dot_general x4, matrix products, per_device(): lax.dot_general(sketch, right, (((0,), (0,)), ((), ())), precision=HIGH,...  15.9 us
    unnamed x7, waiting for transfers between devices  15.4 us
    reduce_scatter x1, waiting for transfers between devices, per_device(): lax.psum_scatter(terms, 'cols', scatter_dimension=1, tiled=True)  13.1 us
  transfers between devices with their start and end apart: 7, of which 7 were waited for; matrix products, arithmetic and copies ran while one was open for 6% of the time, Pallas kernels for 0%

profile of v1, /device:TPU:1, one launch (start us, length us, event | category | flops | bytes accessed | tf_op | source)
XLA Modules:
  0.0 450.5 jit_solution(9941971261360289511)
XLA Ops:
  8.6 1.7 gather_fusion
  10.3 2.2 fusion.12
  12.5 16.3 %all-to-all-start = ((f32[128,16,128]{2,1,0:T(8,128)}), f32[128,16,128]{2,1,0:T(8,128)S(1)}, u32[]{:S(2)}, u32[]{:S(2)}) async-start(f32[128,16,128]{2,1,0:T(8,128)} %bitcast.1), calls=%async_computation | async-start | bytes 2097152 | tf_op jit(solution)/shard_map/all_to_all | solution.py:64
  36.6 1.8 compare_and_fusion
  39.5 16.6 %all-to-all-done = f32[128,16,128]{2,1,0:T(8,128)S(1)} async-done(((f32[128,16,128]{2,1,0:T(8,128)}), f32[128,16,128]{2,1,0:T(8,128)S(1)}, u32[]{:S(2)}, u32[]{:S(2)}) %all-to-all-start) | async-done | bytes 1048608 | tf_op jit(solution)/shard_map/all_to_all | solution.py:64
  65.7 4.9 %fusion = f32[2048,256]{1,0:T(8,128)} fusion(f32[2048,128]{1,0:T(8,128)S(1)} %copy-done.14, f32[2048,128]{1,0:T(8,128)S(1)} %copy-done.13, f32[2048,128]{1,0:T(8,128)S(1)} %get-tuple-element.19, f32[2048,128]{1,0:T(8,128)S(1)} %get-tuple-element.20, f32[128,256]{1,0:T(8,128)S(1)} %get-tuple-element.6, f32[128,256]{1,0:T(8,128)S(1)} %get-tuple-element.7, ...), kind=kOutput, calls=%fused_computation.5 | convolution fusion | flops 3224764416 | bytes 6815744 | tf_op jit(solution)/shard_map/dot_general | solution.py:39
  70.6 13.1 %reduce-scatter.5.cloned.1.call-done = f32[2048,128]{1,0:T(8,128)} async-done(((f32[2048,256]{1,0:T(8,128)}), f32[2048,128]{1,0:T(8,128)}) %reduce-scatter.5.cloned.1.call-update) | async-done | bytes 1048592 | tf_op jit(solution)/shard_map/reduce_scatter | solution.py:70
  83.7 19.0 %all-gather.2.cloned.1.call-done = f32[2048,256]{1,0:T(8,128)} async-done(((f32[2048,128]{1,0:T(8,128)}), f32[2048,256]{1,0:T(8,128)}) %all-gather.2.cloned.1.call-update) | async-done | bytes 2097168 | tf_op jit(solution)/shard_map/all_gather | solution.py:71
  102.7 4.1 fusion.10
  107.4 5.4 %convolution_multiply_fusion.18 = f32[256,128]{1,0:T(8,128)S(1)} fusion(f32[2048,256]{1,0:T(8,128)} %all-gather.2.cloned.1.call-done, f32[2048,128]{1,0:T(8,128)} %bitcast.115, f32[]{:T(128)S(6)} %sub.57), kind=kOutput, calls=%fused_computation.46 | convolution fusion | flops 805339136 | bytes 3276804 | tf_op jit(solution)/shard_map/dot_general | solution.py:87
  112.8 3.4 convolution_multiply_fusion.17
  116.2 3.4 convolution_multiply_fusion.16
  119.7 3.6 convolution_multiply_fusion.15
  124.1 13.2 %all-reduce.5.cloned.1.call-done = f32[256,256]{1,0:T(8,128)} async-done(((f32[256,256]{1,0:T(8,128)}), f32[256,256]{1,0:T(8,128)}) %all-reduce.5.cloned.1.call-update) | async-done | bytes 262160 | tf_op jit(solution)/shard_map/psum | solution.py:79
  137.4 221.3 %all-reduce.9.cloned.1.call-done = (f32[256,256]{1,0:T(8,128)}, f32[256,512]{1,0:T(8,128)}) async-done(((f32[256,256]{1,0:T(8,128)}, f32[256,512]{1,0:T(8,128)}), (f32[256,256]{1,0:T(8,128)}, f32[256,512]{1,0:T(8,128)})) %all-reduce.9.cloned.1.call-update) | async-done | bytes 786448 | tf_op jit(solution)/shard_map/psum | solution.py:79
  358.7 1.6 multiply_reduce_fusion.1
  373.5 1.6 gather_fusion.1
  375.1 29.8 %all-reduce.7.cloned.1.call-done = f32[256,256]{1,0:T(8,128)} async-done(((f32[256,256]{1,0:T(8,128)}), f32[256,256]{1,0:T(8,128)}) %all-reduce.7.cloned.1.call-update) | async-done | bytes 262160 | tf_op jit(solution)/shard_map/psum | solution.py:107
  405.0 1.6 multiply_reduce_fusion
  419.9 1.8 fusion.72
  422.7 1.5 fusion.8
  424.2 2.0 div.43
  426.3 15.3 %reduce-scatter.7.cloned.1.call-done = f32[1024,1]{1,0:T(8,128)} async-done(((f32[2048,1]{1,0:T(8,128)}), f32[1024,1]{1,0:T(8,128)}) %reduce-scatter.7.cloned.1.call-update) | async-done | bytes 4112
  441.6 1.8 copy.11
  (129 shorter events, 44.2 us)
Async XLA Ops:
  7.2 3.1 copy-start
  10.3 18.6 %copy-start.18 = (f32[3]{0:T(128)S(1)}, f32[3]{0:T(128)}, u32[]{:S(2)}) copy-start(f32[3]{0:T(128)} %param.14) | copy-start | bytes 40
  10.3 22.6 %copy-start.19 = (s32[3]{0:T(128)S(1)}, s32[3]{0:T(128)}, u32[]{:S(2)}) copy-start(s32[3]{0:T(128)} %param.13) | copy-start | bytes 40
  10.3 28.1 %copy-start.17 = (s32[1024]{0:T(1024)S(1)}, s32[1024]{0:T(1024)}, u32[]{:S(2)}) copy-start(s32[1024]{0:T(1024)} %param.15) | copy-start | bytes 12292
  12.5 43.6 %all-to-all-start = ((f32[128,16,128]{2,1,0:T(8,128)}), f32[128,16,128]{2,1,0:T(8,128)S(1)}, u32[]{:S(2)}, u32[]{:S(2)}) async-start(f32[128,16,128]{2,1,0:T(8,128)} %bitcast.1), calls=%async_computation | async-start | bytes 2097152 | tf_op jit(solution)/shard_map/all_to_all | solution.py:64
  28.8 54.8 %reduce-scatter.5.cloned.1.call-start = ((), (), s32[]{:S(2)}) async-start(), calls=%async_computation.3 | async-start | bytes 3145728 | tf_op jit(solution)/shard_map/reduce_scatter | solution.py:70
  56.1 7.7 %copy-start.2 = (f32[128,16,128]{2,1,0:T(8,128)}, f32[128,16,128]{2,1,0:T(8,128)S(1)}, u32[]{:S(2)}) copy-start(f32[128,16,128]{2,1,0:T(8,128)S(1)} %all-to-all-done) | copy-start | bytes 3145732
  61.7 1.8 copy-start.20
  63.7 1.6 copy-start.13
  63.8 1.9 copy-start.14
  63.8 1.9 copy-start.16
  70.6 32.2 %all-gather.2.cloned.1.call-start = ((), (), s32[]{:S(2)}) async-start(), calls=%async_computation.4 | async-start | bytes 3145728 | tf_op jit(solution)/shard_map/all_gather | solution.py:71
  83.7 53.6 %all-reduce.5.cloned.1.call-start = ((), (), s32[]{:S(2)}) async-start(), calls=%async_computation.5 | async-start | bytes 524288 | tf_op jit(solution)/shard_map/psum | solution.py:79
  106.8 5.9 %copy-start.1 = (f32[2048,256]{1,0:T(8,128)S(1)}, f32[2048,256]{1,0:T(8,128)}, u32[]{:S(2)}) copy-start(f32[2048,256]{1,0:T(8,128)} %all-gather.2.cloned.1.call-done) | copy-start | bytes 6291460
  106.8 251.9 %all-reduce.9.cloned.1.call-start = ((), (), s32[]{:S(2)}) async-start(), calls=%async_computation.8 | async-start | bytes 1572864 | tf_op jit(solution)/shard_map/psum | solution.py:79
  107.4 5.4 %copy-start.8 = (f32[128,16,128]{2,1,0:T(8,128)S(1)}, f32[128,16,128]{2,1,0:T(8,128)}, u32[]{:S(2)}) copy-start(f32[128,16,128]{2,1,0:T(8,128)} %copy-done.7) | copy-start | bytes 3145732
  112.7 3.5 copy-start.4
  116.2 3.5 copy-start.6
  119.7 17.7 %copy-start.21 = (s32[1,32]{1,0:T(1,128)S(1)}, s32[1,32]{1,0:T(1,128)}, u32[]{:S(2)}) copy-start(s32[1,32]{1,0:T(1,128)} %param.17) | copy-start | bytes 388
  137.4 267.6 %all-reduce.7.cloned.1.call-start = ((), (), s32[]{:S(2)}) async-start(), calls=%async_computation.6 | async-start | bytes 524288 | tf_op jit(solution)/shard_map/psum | solution.py:107
  368.6 2.7 copy-start.15
  369.8 3.8 copy-start.11
  373.2 68.3 %reduce-scatter.7.cloned.1.call-start = ((), (), s32[]{:S(2)}) async-start(), calls=%async_computation.7 | async-start | bytes 1572864
  418.5 4.3 copy-start.10
  (5 other events, 4.6 us)
Sparse Core Ops, SparseCore 0:
  70.7 12.9 reduce-scatter.4
  85.6 17.0 all-gather.1
  107.0 30.3 all-reduce.4
  143.3 215.3 all-reduce.8
  373.4 31.5 all-reduce.6
  426.4 15.1 reduce-scatter.6
